TPU v7x, 256 devices: a whole 4x4x8 slice. The times are simulated.
256 devices in a mesh: section: 2 (over core), srv: 32 (over x, z), tp: 4 (over y).
Axes of the slice: x: 4, y: 4, z: 8, core: 2. Of those that a mesh axis runs over, the one named last changes fastest.
Arguments:
- queries: bfloat16 [8192, 4096], P(('section', 'srv'), 'tp'), may hold values from -40 to 40
- keys: bfloat16 [8192, 512], P(('section', 'srv'), 'tp'), may hold values from -40 to 40
- values: bfloat16 [8192, 512], P(('section', 'srv'), 'tp'), may hold values from -6 to 6
- residual: bfloat16 [8192, 4096], P(('section', 'srv'), 'tp'), may hold values from -6 to 6
- out_weight: bfloat16 [4096, 4096], P('tp', ('section', 'srv')), may hold values from -0.1875 to 0.1875
- norm_gain: float32 [4096], P('tp'), may hold values from 0.25 to 1.75
- level_shift: float32 [8, 4096], P(None, 'tp'), may hold values from -3 to 3
- doc_lengths: int32 [2, 4], P('section'), may hold values from 1 to 128, 256 in all within a row
- noise_level: int32 [2, 4], P('section'), may hold values from 0 to 7
Outputs:
- normed: bfloat16 [8192, 4096], P(('section', 'srv'), 'tp')
Inputs may be any that keep to these rules, and one draw needn't show every extreme that they name: `doc_lengths`: each micro-batch's lengths sum to 256.
All inputs are finite; a program needn't handle non-finite values.
Results may differ from a plain program's by a relative error of at most 0.013.
Values may be sent and summed in bfloat16 or wider, within the bound.
A program may use at most 64 MiB of HBM per device.

v0:
```python
import jax
import jax.numpy as jnp
from jax import lax
from jax.sharding import PartitionSpec as P

D = 4096
HEAD_SIZE = 128
BLK = 16


def in_one_piece(arrays, axis, dim, along):
    ends, at = ([], 0)
    for a in arrays[:-1]:
        at += a.shape[along]
        ends.append(at)
    both = jnp.concatenate(arrays, axis=along)
    return tuple(jnp.split(lax.all_gather(both, axis, axis=dim, tiled=True), ends, axis=along))


def in_blocks(value, dim, length):
    dims = value.shape
    parts = value.reshape(*dims[:dim], length, dims[dim] // length, *dims[dim + 1 :])
    return jnp.moveaxis(parts, dim, 0)


def sent_and_summed(value, axis, dim):
    length = lax.axis_size(axis)
    parts = lax.all_to_all(in_blocks(value, dim, length), axis, 0, 0, tiled=True)
    return jnp.sum(parts.astype(jnp.float32), axis=0)


def from_everyone(value, axis):
    copies = jnp.broadcast_to(value, (lax.axis_size(axis), *value.shape))
    return lax.all_to_all(copies, axis, split_axis=0, concat_axis=0, tiled=True)


def of_everyone(value, axis):
    everything = from_everyone(value, axis)
    return jnp.sum(everything, axis=0)


def bounds(positions, starts, ends):
    member = (positions[:, None] >= starts[None, :]) & (positions[:, None] < ends[None, :])
    first = jnp.sum(jnp.where(member, starts[None, :], 0), axis=1)
    limit = (positions // BLK + 1) * BLK
    return (member, first, limit)


def make_absorb(query_block, first, limit, kv_heads, query_groups):
    rows = query_block.shape[0]
    scale = HEAD_SIZE ** (-0.5)
    grouped = (
        query_block.reshape(rows, kv_heads, query_groups, HEAD_SIZE)
        .transpose(1, 2, 0, 3)
        .reshape(kv_heads, query_groups * rows, HEAD_SIZE)
    )
    row_first = jnp.tile(first, query_groups)
    row_limit = jnp.tile(limit, query_groups)
    empty = (
        jnp.full((kv_heads, query_groups * rows), -1e30, jnp.float32),
        jnp.zeros((kv_heads, query_groups * rows), jnp.float32),
        jnp.zeros((kv_heads, query_groups * rows, HEAD_SIZE), jnp.float32),
    )

    def absorb(carry, pieces, start):
        key_piece, value_piece = pieces
        count = key_piece.shape[0]
        key_pos = jnp.arange(count, dtype=jnp.int32)
        mask = (key_pos[None, :] >= row_first[:, None]) & (key_pos[None, :] < row_limit[:, None])

        def update(state):
            best, total, summed = state
            key_heads = key_piece.reshape(count, kv_heads, HEAD_SIZE)
            value_heads = value_piece.reshape(count, kv_heads, HEAD_SIZE)
            scores = (
                jnp.einsum("kxd,jkd->kxj", grouped, key_heads, preferred_element_type=jnp.float32)
                * scale
            )
            scores = jnp.where(mask[None], scores, -1e30)
            new_best = jnp.maximum(best, jnp.max(scores, axis=-1))
            weights = jnp.where(mask[None], jnp.exp(scores - new_best[..., None]), 0.0)
            total = jnp.sum(weights, axis=-1)
            update_sum = jnp.einsum(
                "kxj,jkd->kxd",
                weights.astype(jnp.bfloat16),
                value_heads,
                preferred_element_type=jnp.float32,
            )
            return (new_best, total, update_sum)

        return lax.cond(jnp.any(mask), update, lambda state: state, carry)

    return (absorb, empty)


def finish(carry, rows, kv_heads, query_groups):
    best, total, summed = carry
    attended = (
        (summed / total[..., None])
        .reshape(kv_heads, query_groups, rows, HEAD_SIZE)
        .transpose(2, 0, 1, 3)
    )
    return attended.reshape(rows, kv_heads * query_groups * HEAD_SIZE).astype(jnp.bfloat16)


def on_device(
    queries, keys, values, residual, out_weight, norm_gain, level_shift, doc_lengths, noise_level
):
    rows = queries.shape[0]
    kv_heads = keys.shape[1] // HEAD_SIZE
    query_groups = queries.shape[1] // keys.shape[1]
    here = lax.axis_index("srv")
    lengths = doc_lengths[0] * BLK
    ends = jnp.cumsum(lengths)
    starts = ends - lengths
    positions = here * rows + jnp.arange(rows, dtype=jnp.int32)
    member, first, limit = bounds(positions, starts, ends)
    absorb, empty = make_absorb(queries, first, limit, kv_heads, query_groups)
    carry = absorb(empty, in_one_piece((keys, values), "srv", 0, 1), jnp.int32(0))
    attended = finish(carry, rows, kv_heads, query_groups)
    partial_sum = jnp.dot(
        attended,
        lax.all_gather(out_weight, ("section", "srv"), axis=1, tiled=True),
        preferred_element_type=jnp.float32,
    )
    share = sent_and_summed(partial_sum.astype(jnp.bfloat16), "tp", 1)
    hidden = residual.astype(jnp.float32) + share
    squares = of_everyone(jnp.sum(hidden * hidden, axis=1), "tp")
    inverse = lax.rsqrt(squares / D + 1e-06)
    level = jnp.sum(jnp.where(member, noise_level[0][None, :], 0), axis=1)
    onehot = (level[:, None] == jnp.arange(level_shift.shape[0], dtype=jnp.int32)[None, :]).astype(
        jnp.float32
    )
    shift = jnp.dot(onehot, level_shift)
    normed = hidden * inverse[:, None] * norm_gain[None, :] * (1.0 + shift)
    return normed.astype(jnp.bfloat16)


def solution(mesh):
    placed = (
        P(("section", "srv"), "tp"),
        P(("section", "srv"), "tp"),
        P(("section", "srv"), "tp"),
        P(("section", "srv"), "tp"),
        P("tp", ("section", "srv")),
        P("tp"),
        P(None, "tp"),
        P("section", None),
        P("section", None),
    )
    return jax.shard_map(
        on_device,
        mesh=mesh,
        in_specs=placed,
        out_specs=P(("section", "srv"), "tp"),
        check_vma=False,
    )
```

profile of v0, /device:TPU:32, one launch (start us, length us, event | category | flops | bytes accessed | tf_op | source)
XLA Modules:
  0.0 215.3 jit_solution(1870984475952749132)
XLA Ops:
  6.5 0.0 copy-start
  6.5 0.0 all-gather.3.cloned.1.call-start
  6.5 1.4 pad_maximum_fusion
  8.0 0.0 all-gather.3.cloned.1.call-update
  8.0 0.0 all-gather.5.cloned.1.call-start
  8.0 0.7 all-gather.5.cloned.1.call-update
  8.7 1.1 copy.23
  9.9 0.7 multiply_bitcast_fusion
  10.5 0.2 reduce-window.4
  10.7 0.7 fusion.18
  11.4 0.7 select_reduce_fusion
  12.1 8.8 %fusion.14 = (pred[1024,4096]{1,0:T(32,128)(4,1)}, pred[]{:T(512)}) fusion(s32[1024]{0:T(1024)S(1)} %broadcast_bitcast_fusion, s32[1024]{0:T(1024)S(1)} %broadcast_bitcast_fusion.1), kind=kLoop, calls=%fused_computation.16 | loop fusion | flops 16777215 | bytes 4202497 | tf_op jit(solution)/shard_map/and | solution.py:69
  21.6 67.9 %all-gather.3.cloned.1.call-done = bf16[4096,256]{1,0:T(8,128)(2,1)} async-done(((bf16[128,256]{1,0:T(8,128)(2,1)}), bf16[4096,256]{1,0:T(8,128)(2,1)}) %all-gather.3.cloned.1.call-update) | async-done | bytes 2097168 | tf_op jit(solution)/shard_map/all_gather | solution.py:17
  89.5 16.3 %conditional.1 = (f32[1,1024]{1,0:T(1,128)S(1)}, f32[1,1024,128]{2,1,0:T(8,128)S(1)}) conditional(s32[]{:T(128)} %convert_element_type.33, () %tuple.13, (bf16[1,8,128,128]{2,3,1,0:T(8,128)(2,1)S(1)}, bf16[4096,256]{1,0:T(8,128)(2,1)}, pred[1024,4096]{1,0:T(32,128)(4,1)}) %tuple.30), branch_computations={%region_3.4_spmd, %region_4.7_spmd} | conditional | flops 2202008576 | bytes 91512904 | solution.py:91
  89.5 0.2 copy.24
  89.7 6.0 %fusion = (f32[1024]{0:T(1024)S(1)}, f32[1024,4096]{1,0:T(8,128)S(1)}) fusion(pred[1024,4096]{1,0:T(32,128)(4,1)} %get-tuple-element.15, bf16[1024,128]{1,0:T(8,128)(2,1)S(1)} %bitcast.40, bf16[4096,256]{1,0:T(8,128)(2,1)} %get-tuple-element.17), kind=kOutput, calls=%fused_computation.2 | convolution fusion | flops 1086323712 | bytes 22286336 | tf_op jit(solution)/shard_map/cond/branch_1_fun/kxd,jkd->kxj/dot_general | solution.py:76
  95.7 0.0 copy-done.3
  95.7 0.0 copy-done.1
  95.7 4.3 %fusion.5 = f32[1,1024,128]{2,1,0:T(8,128)S(1)} fusion(pred[1024,4096]{1,0:T(32,128)(4,1)S(1)} %copy-done.1, f32[1024,4096]{1,0:T(8,128)S(1)} %get-tuple-element.40, f32[1024]{0:T(1024)S(1)} %broadcast_maximum_fusion, bf16[4096,256]{1,0:T(8,128)(2,1)S(1)} %copy-done.3), kind=kOutput, calls=%fused_computation.6 | convolution fusion | flops 1094713344 | bytes 22548480 | tf_op jit(solution)/shard_map/cond/branch_1_fun/kxj,jkd->kxd/dot_general | solution.py:83
  100.0 5.6 %fusion.2 = f32[1024]{0:T(1024)S(1)} fusion(pred[1024,4096]{1,0:T(32,128)(4,1)S(1)} %copy-done.1, f32[1024,4096]{1,0:T(8,128)S(1)} %get-tuple-element.40, f32[1024]{0:T(1024)S(1)} %broadcast_maximum_fusion), kind=kLoop, calls=%fused_computation.4 | loop fusion | flops 20970496 | bytes 20979712 | tf_op jit(solution)/shard_map/cond/branch_1_fun/reduce_sum | solution.py:82
  105.8 0.0 copy-start.2
  105.8 0.0 copy-start.4
  105.8 0.2 divide_convert_fusion
  106.0 0.2 copy.25
  106.2 67.3 %all-gather.5.cloned.1.call-done = bf16[1024,4096]{0,1:T(8,128)(2,1)} async-done(((bf16[1024,64]{0,1:T(8,128)(2,1)}), bf16[1024,4096]{0,1:T(8,128)(2,1)}) %all-gather.5.cloned.1.call-update) | async-done | bytes 8388624 | tf_op jit(solution)/shard_map/all_gather | solution.py:123
  173.5 6.3 %convolution_convert_fusion = bf16[128,4096]{1,0:T(8,128)(2,1)S(1)} fusion(bf16[128,1024]{0,1:T(8,128)(2,1)S(1)} %bitcast.41, bf16[1024,4096]{0,1:T(8,128)(2,1)} %all-gather.5.cloned.1.call-done), kind=kOutput, calls=%fused_computation.17 | convolution fusion | flops 1074266112 | bytes 9699328 | tf_op jit(solution)/shard_map/dot_general | solution.py:121
  179.8 0.1 copy.30
  179.9 19.6 %all_to_all.11 = bf16[4,128,1024]{2,1,0:T(8,128)(2,1)S(1)} all-to-all(bf16[4,128,1024]{2,1,0:T(8,128)(2,1)S(1)} %bitcast.39), channel_id=1, replica_groups=mesh['section'=2,'srv'=32,'tp'=4] {'tp'}, dimensions={0} | all-to-all | bytes 2097152 | tf_op jit(solution)/shard_map/all_to_all | solution.py:28
  199.5 0.2 convert_reduce_fusion
  199.7 0.2 multiply_reduce_fusion
  199.9 7.6 %all_to_all.12 = f32[4,1,128]{2,1,0:T(1,128)S(1)} all-to-all(f32[4,1,128]{2,1,0:T(1,128)S(1)} %broadcast_in_dim.53), channel_id=1, replica_groups=mesh['section'=2,'srv'=32,'tp'=4] {'tp'}, dimensions={0} | all-to-all | bytes 4096 | tf_op jit(solution)/shard_map/all_to_all | solution.py:34
  207.5 1.0 fusion.16
  (12 shorter events, 0.1 us)
Async XLA Ops:
  6.5 201.0 %copy-start = (f32[8,1024]{1,0:T(8,128)S(1)}, f32[8,1024]{1,0:T(8,128)}, u32[]{:S(2)}) copy-start(f32[8,1024]{1,0:T(8,128)} %param.17) | copy-start | bytes 98308
  6.5 83.0 %all-gather.3.cloned.1.call-start = ((), (), s32[]{:S(2)}) async-start(), calls=%async_computation.2 | async-start | bytes 2162688 | tf_op jit(solution)/shard_map/all_gather | solution.py:17
  8.0 165.5 %all-gather.5.cloned.1.call-start = ((), (), s32[]{:S(2)}) async-start(), calls=%async_computation.3 | async-start | bytes 8519680 | tf_op jit(solution)/shard_map/all_gather | solution.py:123
  89.5 6.2 %copy-start.3 = (bf16[4096,256]{1,0:T(8,128)(2,1)S(1)}, bf16[4096,256]{1,0:T(8,128)(2,1)}, u32[]{:S(2)}) copy-start(bf16[4096,256]{1,0:T(8,128)(2,1)} %get-tuple-element.17) | copy-start | bytes 6291460 | tf_op jit(solution)/shard_map/cond
  89.7 6.0 %copy-start.1 = (pred[1024,4096]{1,0:T(32,128)(4,1)S(1)}, pred[1024,4096]{1,0:T(32,128)(4,1)}, u32[]{:S(2)}) copy-start(pred[1024,4096]{1,0:T(32,128)(4,1)} %get-tuple-element.15) | copy-start | bytes 12582916 | tf_op jit(solution)/shard_map/cond
  105.8 93.9 %copy-start.2 = (bf16[128,1024]{1,0:T(8,128)(2,1)S(1)}, bf16[128,1024]{1,0:T(8,128)(2,1)}, u32[]{:S(2)}) copy-start(bf16[128,1024]{1,0:T(8,128)(2,1)} %param.14) | copy-start | bytes 786436
  105.8 101.7 %copy-start.4 = (f32[1024]{0:T(1024)S(1)}, f32[1024]{0:T(1024)}, u32[]{:S(2)}) copy-start(f32[1024]{0:T(1024)} %param.16) | copy-start | bytes 12292
Sparse Core Ops, SparseCore 0:
  10.0 79.5 all-gather.2
  92.3 81.2 all-gather.4
where the time goes:
time: 216 us; the launch traced here: 215 us
  waiting for transfers between devices  136 us (63%)
  blocking collectives  27.2 us (13%)
  other arithmetic  18.6 us (9%)
  matrix products  17.5 us (8%)
  between operations  14.2 us (7%)
    all_gather x1, waiting for transfers between devices, in_one_piece(): lax.all_gather(both, axis, axis=dim, tiled=True)  67.9 us
    all_gather x1, waiting for transfers between devices, on_device(): lax.all_gather(out_weight, ('section', 'srv'), axis=1, tiled=True)  67.3 us
    all_to_all x1, blocking collectives, sent_and_summed(): lax.all_to_all(in_blocks(value, dim, length), axis, 0, 0, tiled=True)  19.6 us
    and x1, other arithmetic, absorb(): (key_pos[None, :] >= row_first[:, None]) & (key_pos[None, :] < row_limit[...  8.79 us
    all_to_all x1, blocking collectives, from_everyone(): return lax.all_to_all(copies, axis, split_axis=0, concat_axis=0, tiled=True)  7.59 us
    dot_general x1, matrix products, on_device(): jnp.dot(attended, lax.all_gather(out_weight, ('section', 'srv'), axis=1,...  6.28 us
    dot_general x1, matrix products, update(): jnp.einsum('kxd,jkd->kxj', grouped, key_heads, preferred_element_type=jnp...  5.97 us
    reduce_sum x1, other arithmetic, update(): total = jnp.sum(weights, axis=-1)  5.58 us
  transfers between devices with their start and end apart: 2, of which 2 were waited for; matrix products, arithmetic and copies ran while one was open for 13% of the time, Pallas kernels for 0%

commit v1 on v0

--- a/solution.py
+++ b/solution.py
@@ -1,11 +1,26 @@
+import functools
 import jax
 import jax.numpy as jnp
 from jax import lax
 from jax.sharding import PartitionSpec as P
+from jax.lax import all_to_all, axis_size
 
 D = 4096
 HEAD_SIZE = 128
 BLK = 16
+
+
+def tell_lane(arr, bus_axis):
+    top = jnp.concatenate(
+        all_to_all(
+            jnp.stack(axis_size(bus_axis) * [arr]), axis_name=bus_axis, split_axis=0, concat_axis=0
+        ),
+        axis=1,
+    )
+    return top
+
+
+recast_the_plane = functools.partial(tell_lane, bus_axis=("section", "srv"))
 
 
 def in_one_piece(arrays, axis, dim, along):
@@ -119,9 +134,7 @@
     carry = absorb(empty, in_one_piece((keys, values), "srv", 0, 1), jnp.int32(0))
     attended = finish(carry, rows, kv_heads, query_groups)
     partial_sum = jnp.dot(
-        attended,
-        lax.all_gather(out_weight, ("section", "srv"), axis=1, tiled=True),
-        preferred_element_type=jnp.float32,
+        attended, recast_the_plane(out_weight), preferred_element_type=jnp.float32
     )
     share = sent_and_summed(partial_sum.astype(jnp.bfloat16), "tp", 1)
     hidden = residual.astype(jnp.float32) + share

time: 216 us -> 269 us (1.25)
  waiting for transfers between devices: 136 us -> 175 us
  starting transfers between devices: 0.04 us -> 12 us
  local copies, waits for them, and re-layouts: 1.6 us -> 5.86 us
  other arithmetic: 18.6 us -> 15.8 us
    all_gather x1 -> x0, waiting for transfers between devices: 67.3 us -> none  [on_device(): lax.all_gather(out_weight, ('section', 'srv'), axis=1, tiled=True)]
    all_to_all x0 -> x1, waiting for transfers between devices: none -> 59.1 us  [tell_lane(): all_to_all(jnp.stack(axis_size(bus_axis) * [arr]), axis_name=bus_axis, sp...]
    all_gather x1, waiting for transfers between devices: 67.9 us -> 116 us  [in_one_piece(): lax.all_gather(both, axis, axis=dim, tiled=True)]
    all_to_all x0 -> x1, starting transfers between devices: none -> 11.9 us  [tell_lane(): all_to_all(jnp.stack(axis_size(bus_axis) * [arr]), axis_name=bus_axis, sp...]
    another operation x1 -> x2, local copies, waits for them, and re-layouts: 0.18 us -> 5.37 us  [the longest x1 5.19 us: tell_lane(): jnp.stack(axis_size(bus_axis) * [arr])]
  transfers between devices with their start and end apart: 2 -> 2, of which waited for: 2 -> 2; matrix products, arithmetic and copies ran while one was open for 13% -> 10% of each run, Pallas kernels for 0% -> 0%
where the time goes in v1:
time: 269 us; the launch traced here: 267 us
  waiting for transfers between devices  175 us (65%)
  blocking collectives  27.1 us (10%)
  matrix products  17.5 us (7%)
  other arithmetic  15.8 us (6%)
  between operations  14.2 us (5%)
  starting transfers between devices  12 us (4%)
  local copies, waits for them, and re-layouts  5.86 us (2%)
    all_gather x1, waiting for transfers between devices, in_one_piece(): lax.all_gather(both, axis, axis=dim, tiled=True)  116 us
    all_to_all x1, waiting for transfers between devices, tell_lane(): all_to_all(jnp.stack(axis_size(bus_axis) * [arr]), axis_name=bus_axis, sp...  59.1 us
    all_to_all x1, blocking collectives, sent_and_summed(): lax.all_to_all(in_blocks(value, dim, length), axis, 0, 0, tiled=True)  19.5 us
    all_to_all x1, starting transfers between devices, tell_lane(): all_to_all(jnp.stack(axis_size(bus_axis) * [arr]), axis_name=bus_axis, sp...  11.9 us
    and x1, other arithmetic, absorb(): (key_pos[None, :] >= row_first[:, None]) & (key_pos[None, :] < row_limit[...  8.72 us
    all_to_all x1, blocking collectives, from_everyone(): return lax.all_to_all(copies, axis, split_axis=0, concat_axis=0, tiled=True)  7.59 us
    dot_general x1, matrix products, on_device(): jnp.dot(attended, recast_the_plane(out_weight), preferred_element_type=jn...  6.28 us
    dot_general x1, matrix products, update(): jnp.einsum('kxd,jkd->kxj', grouped, key_heads, preferred_element_type=jnp...  5.97 us
  transfers between devices with their start and end apart: 2, of which 2 were waited for; matrix products, arithmetic and copies ran while one was open for 10% of the time, Pallas kernels for 0%

profile of v1, /device:TPU:32, one launch (start us, length us, event | category | flops | bytes accessed | tf_op | source)
XLA Modules:
  0.0 267.3 jit_solution(13706088003604370948)
XLA Ops:
  6.5 0.0 copy-start
  6.5 5.2 %stack.2 = bf16[64,1024,64]{1,2,0:T(8,128)(2,1)} broadcast(bf16[1024,64]{0,1:T(8,128)(2,1)} %param.15), dimensions={1,2} | broadcast | bytes 8519680 | tf_op jit(solution)/shard_map/stack | solution.py:16
  11.7 0.0 copy-start.8
  11.8 11.9 %all-to-all-start = ((bf16[64,1024,64]{1,2,0:T(8,128)(2,1)}), bf16[64,1024,64]{1,2,0:T(8,128)(2,1)}, u32[]{:S(2)}, u32[]{:S(2)}) async-start(bf16[64,1024,64]{1,2,0:T(8,128)(2,1)} %stack.2), calls=%async_computation | async-start | bytes 16777216 | tf_op jit(solution)/shard_map/all_to_all | solution.py:15
  23.7 0.0 all-gather.2.cloned.1.call-start
  23.8 0.6 pad_maximum_fusion
  24.4 0.0 all-gather.2.cloned.1.call-update
  24.4 0.0 copy-done.4
  24.4 0.2 copy.24
  24.6 0.2 reduce-window.4
  24.8 0.1 select_reduce_fusion
  24.9 8.7 %fusion.14 = (pred[1024,4096]{1,0:T(32,128)(4,1)}, pred[]{:T(512)}) fusion(s32[1024]{0:T(1024)S(1)} %broadcast_bitcast_fusion, s32[1024]{0:T(1024)S(1)} %broadcast_bitcast_fusion.1), kind=kLoop, calls=%fused_computation.16 | loop fusion | flops 16777215 | bytes 4202497 | tf_op jit(solution)/shard_map/and | solution.py:84
  34.2 115.5 %all-gather.2.cloned.1.call-done = bf16[4096,256]{1,0:T(8,128)(2,1)} async-done(((bf16[128,256]{1,0:T(8,128)(2,1)}), bf16[4096,256]{1,0:T(8,128)(2,1)}) %all-gather.2.cloned.1.call-update) | async-done | bytes 2097168 | tf_op jit(solution)/shard_map/all_gather | solution.py:32
  149.7 16.3 %conditional.1 = (f32[1,1024]{1,0:T(1,128)S(1)}, f32[1,1024,128]{2,1,0:T(8,128)S(1)}) conditional(s32[]{:T(128)} %convert_element_type.33, () %tuple.13, (bf16[1,8,128,128]{2,3,1,0:T(8,128)(2,1)S(1)}, bf16[4096,256]{1,0:T(8,128)(2,1)}, pred[1024,4096]{1,0:T(32,128)(4,1)}) %tuple.28), branch_computations={%region_3.4_spmd, %region_4.7_spmd} | conditional | flops 2202008576 | bytes 91512904 | solution.py:106
  149.7 0.2 copy.25
  149.9 0.0 copy-start.1
  149.9 0.0 copy-start.3
  150.0 6.0 %fusion = (f32[1024]{0:T(1024)S(1)}, f32[1024,4096]{1,0:T(8,128)S(1)}) fusion(pred[1024,4096]{1,0:T(32,128)(4,1)} %get-tuple-element.15, bf16[1024,128]{1,0:T(8,128)(2,1)S(1)} %bitcast.43, bf16[4096,256]{1,0:T(8,128)(2,1)} %get-tuple-element.17), kind=kOutput, calls=%fused_computation.2 | convolution fusion | flops 1086323712 | bytes 22286336 | tf_op jit(solution)/shard_map/cond/branch_1_fun/kxd,jkd->kxj/dot_general | solution.py:91
  156.0 4.3 %fusion.5 = f32[1,1024,128]{2,1,0:T(8,128)S(1)} fusion(pred[1024,4096]{1,0:T(32,128)(4,1)S(1)} %copy-done.1, f32[1024,4096]{1,0:T(8,128)S(1)} %get-tuple-element.40, f32[1024]{0:T(1024)S(1)} %broadcast_maximum_fusion, bf16[4096,256]{1,0:T(8,128)(2,1)S(1)} %copy-done.3), kind=kOutput, calls=%fused_computation.6 | convolution fusion | flops 1094713344 | bytes 22548480 | tf_op jit(solution)/shard_map/cond/branch_1_fun/kxj,jkd->kxd/dot_general | solution.py:98
  160.3 5.6 %fusion.2 = f32[1024]{0:T(1024)S(1)} fusion(pred[1024,4096]{1,0:T(32,128)(4,1)S(1)} %copy-done.1, f32[1024,4096]{1,0:T(8,128)S(1)} %get-tuple-element.40, f32[1024]{0:T(1024)S(1)} %broadcast_maximum_fusion), kind=kLoop, calls=%fused_computation.4 | loop fusion | flops 20970496 | bytes 20979712 | tf_op jit(solution)/shard_map/cond/branch_1_fun/reduce_sum | solution.py:97
  166.0 0.0 copy-start.2
  166.0 0.2 divide_convert_fusion
  166.3 0.0 copy-start.7
  166.3 0.2 copy.26
  166.5 59.1 %all-to-all-done = bf16[64,1024,64]{1,2,0:T(8,128)(2,1)} async-done(((bf16[64,1024,64]{1,2,0:T(8,128)(2,1)}), bf16[64,1024,64]{1,2,0:T(8,128)(2,1)}, u32[]{:S(2)}, u32[]{:S(2)}) %all-to-all-start) | async-done | bytes 8388640 | tf_op jit(solution)/shard_map/all_to_all | solution.py:15
  225.6 6.3 %convolution_convert_fusion = bf16[128,4096]{1,0:T(8,128)(2,1)S(1)} fusion(bf16[128,1024]{0,1:T(8,128)(2,1)S(1)} %bitcast.44, bf16[1024,4096]{0,1:T(8,128)(2,1)} %bitcast.16), kind=kOutput, calls=%fused_computation.17 | convolution fusion | flops 1074266112 | bytes 9699328 | tf_op jit(solution)/shard_map/dot_general | solution.py:136
  231.8 0.1 copy.31
  231.9 19.5 %all_to_all.16 = bf16[4,128,1024]{2,1,0:T(8,128)(2,1)S(1)} all-to-all(bf16[4,128,1024]{2,1,0:T(8,128)(2,1)S(1)} %bitcast.42), channel_id=1, replica_groups=mesh['section'=2,'srv'=32,'tp'=4] {'tp'}, dimensions={0} | all-to-all | bytes 2097152 | tf_op jit(solution)/shard_map/all_to_all | solution.py:43
  251.5 0.2 convert_reduce_fusion
  251.7 0.2 multiply_reduce_fusion
  251.8 7.6 %all_to_all.17 = f32[4,1,128]{2,1,0:T(1,128)S(1)} all-to-all(f32[4,1,128]{2,1,0:T(1,128)S(1)} %broadcast_in_dim.53), channel_id=1, replica_groups=mesh['section'=2,'srv'=32,'tp'=4] {'tp'}, dimensions={0} | all-to-all | bytes 4096 | tf_op jit(solution)/shard_map/all_to_all | solution.py:49
  259.5 1.0 fusion.16
  (22 shorter events, 0.1 us)
Async XLA Ops:
  6.5 252.9 %copy-start = (f32[8,1024]{1,0:T(8,128)S(1)}, f32[8,1024]{1,0:T(8,128)}, u32[]{:S(2)}) copy-start(f32[8,1024]{1,0:T(8,128)} %param.17) | copy-start | bytes 98308
  11.7 12.0 %copy-start.5 = (bf16[128,128]{1,0:T(8,128)(2,1)S(1)}, bf16[128,128]{1,0:T(8,128)(2,1)}, u32[]{:S(2)}) copy-start(bf16[128,128]{1,0:T(8,128)(2,1)} %param.13) | copy-start | bytes 98308
  11.7 12.0 %copy-start.6 = (bf16[128,128]{1,0:T(8,128)(2,1)S(1)}, bf16[128,128]{1,0:T(8,128)(2,1)}, u32[]{:S(2)}) copy-start(bf16[128,128]{1,0:T(8,128)(2,1)} %param.12) | copy-start | bytes 98308
  11.7 12.7 %copy-start.4 = (bf16[128,1024]{1,0:T(8,128)(2,1)S(1)}, bf16[128,1024]{1,0:T(8,128)(2,1)}, u32[]{:S(2)}) copy-start(bf16[128,1024]{1,0:T(8,128)(2,1)} %param.11) | copy-start | bytes 786436
  11.7 12.9 %copy-start.9 = (s32[1,4]{1,0:T(1,128)S(1)}, s32[1,4]{1,0:T(1,128)}, u32[]{:S(2)}) copy-start(s32[1,4]{1,0:T(1,128)} %param.18) | copy-start | bytes 52
  11.7 13.1 %copy-start.8 = (s32[1,4]{1,0:T(1,128)S(1)}, s32[1,4]{1,0:T(1,128)}, u32[]{:S(2)}) copy-start(s32[1,4]{1,0:T(1,128)} %param.19) | copy-start | bytes 52
  11.8 213.8 %all-to-all-start = ((bf16[64,1024,64]{1,2,0:T(8,128)(2,1)}), bf16[64,1024,64]{1,2,0:T(8,128)(2,1)}, u32[]{:S(2)}, u32[]{:S(2)}) async-start(bf16[64,1024,64]{1,2,0:T(8,128)(2,1)} %stack.2), calls=%async_computation | async-start | bytes 16777216 | tf_op jit(solution)/shard_map/all_to_all | solution.py:15
  23.7 126.1 %all-gather.2.cloned.1.call-start = ((), (), s32[]{:S(2)}) async-start(), calls=%async_computation.3 | async-start | bytes 2162688 | tf_op jit(solution)/shard_map/all_gather | solution.py:32
  149.9 6.0 %copy-start.1 = (pred[1024,4096]{1,0:T(32,128)(4,1)S(1)}, pred[1024,4096]{1,0:T(32,128)(4,1)}, u32[]{:S(2)}) copy-start(pred[1024,4096]{1,0:T(32,128)(4,1)} %get-tuple-element.15) | copy-start | bytes 12582916 | tf_op jit(solution)/shard_map/cond
  149.9 6.0 %copy-start.3 = (bf16[4096,256]{1,0:T(8,128)(2,1)S(1)}, bf16[4096,256]{1,0:T(8,128)(2,1)}, u32[]{:S(2)}) copy-start(bf16[4096,256]{1,0:T(8,128)(2,1)} %get-tuple-element.17) | copy-start | bytes 6291460 | tf_op jit(solution)/shard_map/cond
  166.0 85.6 %copy-start.2 = (bf16[128,1024]{1,0:T(8,128)(2,1)S(1)}, bf16[128,1024]{1,0:T(8,128)(2,1)}, u32[]{:S(2)}) copy-start(bf16[128,1024]{1,0:T(8,128)(2,1)} %param.14) | copy-start | bytes 786436
  166.3 93.2 %copy-start.7 = (f32[1024]{0:T(1024)S(1)}, f32[1024]{0:T(1024)}, u32[]{:S(2)}) copy-start(f32[1024]{0:T(1024)} %param.16) | copy-start | bytes 12292
Sparse Core Ops, SparseCore 0:
  27.1 122.5 all-gather.1
